TPU v7x, 256 devices: a whole 4x4x8 slice. The times are simulated.
256 devices in a mesh: seq: 64 (over y, z, core), head: 4 (over x).
Axes of the slice: x: 4, y: 4, z: 8, core: 2. Of those that a mesh axis runs over, the one named last changes fastest.
Arguments:
- inner_input: bfloat16 [16384, 8192], P('seq', 'head'), may hold values from -6 to 6
- state_input: bfloat16 [16384, 2, 1024], P('seq', None, 'head'), may hold values from -3 to 3
- gate_input: bfloat16 [16384, 8192], P('seq', 'head'), may hold values from -6 to 6
- step_input: float32 [128, 16384], P('head', 'seq'), may hold values from -4.7 to 0.6
- decay_exponent: float32 [128], P('head')
- skip_gain: float32 [128], P('head'), may hold values from 0.5 to 1.5
- documents: int32 [16384], P('seq'), may hold values from 0 to 15, never falling along the last dimension, each value on 1 to 1536 neighbouring positions
- filter_inner: float32 [4, 8192], P(None, 'head'), may hold values from -3 to 3
- filter_state: float32 [4, 2, 1024], P(None, None, 'head'), may hold values from -3 to 3
- norm_gain: float32 [8192], P('head'), may hold values from 0.1 to 1.9
- output_weight: bfloat16 [8192, 4096], P('head', 'seq'), may hold values from -0.0625 to 0.0625
Outputs:
- mixed: bfloat16 [16384, 4096], P('seq', 'head')
Inputs may be any that keep to these rules, and one draw needn't show every extreme that they name: `documents`: document numbers never fall along the sequence.
All inputs are finite; a program needn't handle non-finite values.
Results may differ from a plain program's by a relative error of at most 0.0058.
Values may be sent and summed in bfloat16 or wider, within the bound.
No kernel may reach another device: no remote copies, remote signals or barrier semaphores. Data moves between devices by JAX's collectives and lax.ppermute only.
A program may use at most 192 MiB of HBM per device.

v0:
```python
import jax
import jax.numpy as jnp
from jax import lax
from jax.sharding import PartitionSpec as P

HEAD_DIM = 64
STATE = 128
GROUPS = 8
INNER = 8192
KERNEL = 4
SPAN = 256
DOC_MOST = 1536
REACH = -(-(DOC_MOST - 1) // SPAN)
highest = lax.Precision.HIGHEST


def passed_along(value, axis, steps):
    count = lax.axis_size(axis)
    initial, last = (max(0, -steps), min(count, count - steps))
    return lax.ppermute(value, axis, [(source, source + steps) for source in range(initial, last)])


def causal_conv(extended, weights, segments_wide, segment_block):
    length = segment_block.shape[0]
    running = jnp.zeros(extended[:length].shape, jnp.float32)
    for offset in range(KERNEL):
        window = extended[offset : offset + length].astype(jnp.float32)
        matches = segments_wide[offset : offset + length] == segment_block
        matches = matches.reshape((length,) + (1,) * (extended.ndim - 1))
        running = running + jnp.where(matches, window * weights[offset], jnp.float32(0.0))
    return jax.nn.silu(running).astype(jnp.bfloat16)


def span_parts(values, write_rows, read_rows, step_size, decay_rate, segment_block, prior_segment):
    length = segment_block.shape[0]
    repeat = decay_rate.shape[0] // write_rows.shape[1]
    cumulative = jnp.cumsum(decay_rate, axis=1)
    places = jnp.arange(length)
    linked = (segment_block[:, None] == segment_block[None, :]) & (
        places[:, None] >= places[None, :]
    )
    spread = cumulative[:, :, None] - cumulative[:, None, :]
    decays = jnp.exp(jnp.where(linked[None], spread, -jnp.inf))
    scores = jnp.einsum("ign,jgn->gij", read_rows, write_rows, preferred_element_type=jnp.float32)
    scores = jnp.repeat(scores, repeat, axis=0)
    mixing = (decays * scores * step_size[:, None, :]).astype(jnp.bfloat16)
    within = jnp.einsum("hij,jhp->ihp", mixing, values, preferred_element_type=jnp.float32)
    inflow = jnp.exp(cumulative) * (segment_block == prior_segment)[None, :].astype(jnp.float32)
    final_segment = segment_block[-1]
    closing = (
        jnp.exp(cumulative[:, -1:] - cumulative)
        * (segment_block == final_segment)[None, :].astype(jnp.float32)
        * step_size
    )
    weighted = (values.astype(jnp.float32) * closing.T[:, :, None]).astype(jnp.bfloat16)
    writes = jnp.repeat(write_rows, repeat, axis=1)
    deposit = jnp.einsum("jhp,jhn->hpn", weighted, writes, preferred_element_type=jnp.float32)
    fading = jnp.exp(cumulative[:, -1]) * (final_segment == prior_segment).astype(jnp.float32)
    return (within, inflow, fading, deposit)


def reading(read_rows, held_state, repeat):
    readers = jnp.repeat(read_rows, repeat, axis=1).astype(jnp.float32)
    return jnp.einsum("ihn,hpn->ihp", readers, held_state, precision=highest)


def gated_norm(outputs, gates, norm_scale):
    width = INNER // GROUPS
    gated = outputs * jax.nn.silu(gates.astype(jnp.float32))
    pieces = []
    for start in range(0, outputs.shape[1], width):
        group = gated[:, start : start + width]
        mean_square = jnp.mean(group * group, axis=-1, keepdims=True)
        scaled = group * lax.rsqrt(mean_square + 1e-05) * norm_scale[start : start + width]
        pieces.append(scaled.astype(jnp.bfloat16))
    return jnp.concatenate(pieces, axis=1)


def chain_states(fading, deposit):
    half = fading.shape[0] // 2
    count = lax.axis_size("seq")
    swap = [(place, place ^ 1) for place in range(count)]
    second = lax.axis_index("seq") % 2 == 1

    def own(a):
        return jnp.where(second, a[half:], a[:half])

    def partner(a):
        return jnp.where(second, a[:half], a[half:])

    there = own(lax.ppermute(fading, "seq", swap))[:, None, None]
    here = own(fading)[:, None, None]
    other = lax.ppermute(partner(deposit).astype(jnp.bfloat16), "seq", swap).astype(jnp.float32)
    mine = own(deposit)
    early_fade, late_fade = (jnp.where(second, there, here), jnp.where(second, here, there))
    early, late = (jnp.where(second, other, mine), jnp.where(second, mine, other))
    added = late_fade * early + late
    scale = early_fade * late_fade
    carried = passed_along(added.astype(jnp.bfloat16), "seq", 2)
    for _ in range(-(-REACH // 2) - 1):
        held = scale * carried.astype(jnp.float32) + added
        carried = passed_along(held.astype(jnp.bfloat16), "seq", 2)
    first = carried.astype(jnp.float32)
    between = early_fade * first + early
    sent = jnp.where(second, first, between).astype(jnp.bfloat16)
    kept = jnp.where(second, between, first)
    got = lax.ppermute(sent, "seq", swap).astype(jnp.float32)
    return jnp.concatenate([jnp.where(second, got, kept), jnp.where(second, kept, got)])


def on_device(
    inner_input,
    state_input,
    gate_input,
    step_input,
    decay_exponent,
    skip_gain,
    documents,
    filter_inner,
    filter_state,
    norm_gain,
    output_weight,
):
    weight = lax.all_gather(output_weight, "seq", axis=1, tiled=True)
    margin = KERNEL - 1
    length = documents.shape[0]
    head_count = decay_exponent.shape[0]
    groups = state_input.shape[2] // STATE
    repeat = head_count // groups
    channels = inner_input.shape[1]
    state_channels = 2 * state_input.shape[2]
    halo = jnp.concatenate(
        [
            inner_input[-margin:],
            state_input[-margin:].reshape(margin, state_channels),
            jnp.broadcast_to(documents[-margin:, None].astype(jnp.bfloat16), (margin, 128)),
        ],
        axis=1,
    )
    halo = passed_along(halo, "seq", 1)
    before_inner = halo[:, :channels]
    before_state = halo[:, channels : channels + state_channels].reshape(margin, 2, -1)
    before_segments = halo[:, channels + state_channels]
    segments_wide = jnp.concatenate([before_segments.astype(jnp.int32), documents])
    inner_conv = causal_conv(
        jnp.concatenate([before_inner, inner_input]), filter_inner, segments_wide, documents
    )
    state_conv = causal_conv(
        jnp.concatenate([before_state, state_input]), filter_state, segments_wide, documents
    )
    values = inner_conv.reshape(length, head_count, HEAD_DIM)
    write_rows = state_conv[:, 0].reshape(length, groups, STATE)
    read_rows = state_conv[:, 1].reshape(length, groups, STATE)
    step_size = jax.nn.softplus(step_input)
    decay_rate = -step_size * jnp.exp(decay_exponent)[:, None]
    skipped = skip_gain[None, :, None] * values.astype(jnp.float32)
    prior_segment = segments_wide[margin - 1]
    within, inflow, fading, deposit = span_parts(
        values, write_rows, read_rows, step_size, decay_rate, documents, prior_segment
    )
    carried = chain_states(fading, deposit)
    outputs = within + inflow.T[:, :, None] * reading(read_rows, carried, repeat) + skipped
    scan_out = outputs.reshape(length, head_count * HEAD_DIM)
    normed = gated_norm(scan_out, gate_input, norm_gain)
    partial_value = jnp.dot(normed, weight, preferred_element_type=jnp.float32)
    return lax.psum_scatter(
        partial_value.astype(jnp.bfloat16), "head", scatter_dimension=1, tiled=True
    )


def solution(mesh):
    placed = (
        P("seq", "head"),
        P("seq", None, "head"),
        P("seq", "head"),
        P("head", "seq"),
        P("head"),
        P("head"),
        P("seq"),
        P(None, "head"),
        P(None, None, "head"),
        P("head"),
        P("head", "seq"),
    )
    return jax.shard_map(
        on_device, mesh=mesh, in_specs=placed, out_specs=P("seq", "head"), check_vma=False
    )
```

profile of v0, /device:TPU:1, one launch (start us, length us, event | category | flops | bytes accessed | tf_op | source)
XLA Modules:
  0.0 170.2 jit_solution(2397949163513260238)
XLA Ops:
  6.5 0.7 all-gather.2.cloned.1.call-update
  7.3 0.8 slice.128
  8.1 0.7 slice_bitcast_fusion
  8.8 0.7 convert.3
  9.6 4.9 %collective-permute-start = (bf16[3,2688]{1,0:T(4,128)(2,1)S(1)}, bf16[3,2688]{1,0:T(4,128)(2,1)S(1)}, u32[]{:S(2)}, u32[]{:S(2)}) collective-permute-start(bf16[3,2688]{1,0:T(4,128)(2,1)S(1)} %pad_maximum_fusion.2), channel_id=1, source_target_pairs={{0,4},{4,8},{8,12},{12,16},{16,20},{20,24},{24,28},{28,32},{32,36}... | collective-permute-start | bytes 48392 | tf_op jit(solution)/shard_map/ppermute | solution.py:20
  14.6 0.7 exp.32
  15.2 0.8 copy_bitcast_fusion.1
  16.1 0.6 reduce-window.6
  16.8 0.7 slice_bitcast_fusion.4
  17.7 0.9 fusion.32
  18.8 1.3 slice.157
  20.1 1.1 copy.19
  23.4 0.8 pad_add_fusion
  24.1 2.0 %slice_compare_fusion.2 = (pred[256]{0:T(512)(128)(4,1)S(1)}, pred[256]{0:T(512)(128)(4,1)S(1)}, pred[256]{0:T(512)(128)(4,1)S(1)}, f32[256]{0:T(256)S(1)}, f32[256]{0:T(256)S(1)}) fusion(s32[256]{0:T(256)} %param.17, s32[259]{0:T(512)S(1)} %pad_add_fusion, s32[]{:T(128)} %bitcast.14, s32[]{:T(128)} %bitcast.16), kind=kLoop, calls=%fused_computation.81 | loop fusion | flops 1792 | bytes 6920 | tf_op jit(solution)/shard_map/eq | solution.py:28
  26.1 0.7 multiply_convert_fusion.3
  27.1 2.1 %multiply_convert_fusion = bf16[256,2048]{1,0:T(8,128)(2,1)S(1)} fusion(bf16[256,2048]{1,0:T(8,128)(2,1)S(1)} %copy-done, bf16[3,2048]{1,0:T(4,128)(2,1)S(1)} %slice.169, f32[2048]{0:T(1024)S(1)} %bitcast.77, f32[2048]{0:T(1024)S(1)} %bitcast.78, f32[2048]{0:T(1024)S(1)} %bitcast.76, f32[2048]{0:T(1024)S(1)} %bitcast.75, ...), kind=kLoop, calls=%fused_computation.16 | loop fusion | flops 14680064 | bytes 2142976 | tf_op jit(solution)/shard_map/convert_element_type | solution.py:31
  29.8 0.7 multiply_bitcast_fusion.1
  32.1 1.0 collective-permute-done.1
  33.4 3.7 %collective-permute-start.3 = (bf16[16,64,128]{2,1,0:T(8,128)(2,1)S(1)}, bf16[16,64,128]{2,1,0:T(8,128)(2,1)S(1)}, u32[]{:S(2)}, u32[]{:S(2)}) collective-permute-start(bf16[16,64,128]{2,1,0:T(8,128)(2,1)S(1)} %get-tuple-element.9), channel_id=1, source_target_pairs={{0,8},{4,12},{8,16},{12,20},{16,24},{20,28},{24,32},{28,36},{32,40... | collective-permute-start | bytes 786440 | tf_op jit(solution)/shard_map/ppermute | solution.py:20
  37.1 9.5 %collective-permute-done.3 = bf16[16,64,128]{2,1,0:T(8,128)(2,1)S(1)} collective-permute-done((bf16[16,64,128]{2,1,0:T(8,128)(2,1)S(1)}, bf16[16,64,128]{2,1,0:T(8,128)(2,1)S(1)}, u32[]{:S(2)}, u32[]{:S(2)}) %collective-permute-start.3) | collective-permute-done | bytes 262176 | tf_op jit(solution)/shard_map/ppermute | solution.py:20
  46.8 4.2 %collective-permute-start.4 = (bf16[16,64,128]{2,1,0:T(8,128)(2,1)S(1)}, bf16[16,64,128]{2,1,0:T(8,128)(2,1)S(1)}, u32[]{:S(2)}, u32[]{:S(2)}) collective-permute-start(bf16[16,64,128]{2,1,0:T(8,128)(2,1)S(1)} %add_convert_fusion.1), channel_id=1, source_target_pairs={{0,8},{4,12},{8,16},{12,20},{16,24},{20,28},{24,32},{28,36},{32,40... | collective-permute-start | bytes 786440 | tf_op jit(solution)/shard_map/ppermute | solution.py:20
  51.2 5.1 %collective-permute-done.4 = bf16[16,64,128]{2,1,0:T(8,128)(2,1)S(1)} collective-permute-done((bf16[16,64,128]{2,1,0:T(8,128)(2,1)S(1)}, bf16[16,64,128]{2,1,0:T(8,128)(2,1)S(1)}, u32[]{:S(2)}, u32[]{:S(2)}) %collective-permute-start.4) | collective-permute-done | bytes 262176 | tf_op jit(solution)/shard_map/ppermute | solution.py:20
  56.5 4.1 %collective-permute-start.5 = (bf16[16,64,128]{2,1,0:T(8,128)(2,1)S(1)}, bf16[16,64,128]{2,1,0:T(8,128)(2,1)S(1)}, u32[]{:S(2)}, u32[]{:S(2)}) collective-permute-start(bf16[16,64,128]{2,1,0:T(8,128)(2,1)S(1)} %add_convert_fusion), channel_id=1, source_target_pairs={{0,8},{4,12},{8,16},{12,20},{16,24},{20,28},{24,32},{28,36},{32,40... | collective-permute-start | bytes 786440 | tf_op jit(solution)/shard_map/ppermute | solution.py:20
  61.1 2.4 %fusion.1 = bf16[32,256,256]{2,1,0:T(8,128)(2,1)S(1)} fusion(f32[32,256]{1,0:T(8,128)S(1)} %copy-done.5, f32[2,256,256]{2,1,0:T(8,128)S(1)} %fusion.34, f32[32,256]{1,0:T(8,128)S(1)} %copy-done.3, pred[256,256]{1,0:T(8,128)(4,1)S(1)} %fusion.25), kind=kLoop, calls=%fused_computation.2 | loop fusion | flops 10485760 | bytes 4849664 | tf_op jit(solution)/shard_map/convert_element_type | solution.py:46
  63.5 0.9 collective-permute-done.5
  64.5 6.5 %collective-permute-start.6 = (bf16[16,64,128]{2,1,0:T(8,128)(2,1)S(1)}, bf16[16,64,128]{2,1,0:T(8,128)(2,1)S(1)}, u32[]{:S(2)}, u32[]{:S(2)}) collective-permute-start(bf16[16,64,128]{2,1,0:T(8,128)(2,1)S(1)} %fusion.22), channel_id=1, source_target_pairs={{0,4},{4,0},{8,12},{12,8},{16,20},{20,16},{24,28},{28,24},{32,36},... | collective-permute-start | bytes 786440 | tf_op jit(solution)/shard_map/ppermute | solution.py:107
  71.0 1.4 fusion.35
  73.2 3.6 %fusion.3 = f32[256,32,64]{0,2,1:T(8,128)} fusion(bf16[256,32,64]{0,2,1:T(8,128)(2,1)S(1)} %bitcast.66, f32[32,64,256]{2,1,0:T(8,128)S(1)} %fusion.35, bf16[256,32,128]{2,0,1:T(8,128)(2,1)S(1)} %bitcast.68, f32[16,64,128]{2,1,0:T(8,128)S(1)} %get-tuple-element.14, f32[16,64,128]{2,1,0:T(8,128)S(1)} %get-tuple-element.13, f32[32]{0:T(128)S(1)} %copy-done.9, ...), kind=kOutput, calls=%fused_computation.9 | convolution fusion | flops 808189952 | bytes 8421504 | tf_op jit(solution)/shard_map/ihn,hpn->ihp/dot_general | solution.py:64
  76.8 2.2 %copy.25 = f32[256,2048]{1,0:T(8,128)S(1)} copy(f32[256,2048]{0,1:T(8,128)} %bitcast.69) | data formatting | bytes 4194304 | tf_op jit(solution)/shard_map/reshape | solution.py:163
  80.1 35.4 %all-gather.2.cloned.1.call-done = bf16[2048,4096]{0,1:T(8,128)(2,1)} async-done(((bf16[2048,64]{0,1:T(8,128)(2,1)}), bf16[2048,4096]{0,1:T(8,128)(2,1)}) %all-gather.2.cloned.1.call-update) | async-done | bytes 16777232 | tf_op jit(solution)/shard_map/all_gather | solution.py:124
  115.4 18.1 %convolution_convert_fusion = bf16[256,4096]{1,0:T(8,128)(2,1)} fusion(bf16[2048,4096]{0,1:T(8,128)(2,1)} %all-gather.2.cloned.1.call-done, bf16[256,1024]{1,0:T(8,128)(2,1)S(1)} %get-tuple-element.12, bf16[256,1024]{1,0:T(8,128)(2,1)S(1)} %get-tuple-element.11), kind=kOutput, calls=%fused_computation.3 | convolution fusion | flops 4298113024 | bytes 19922944 | tf_op jit(solution)/shard_map/dot_general | solution.py:165
  133.5 29.8 %reduce-scatter.2.cloned.1.call-done = bf16[256,1024]{1,0:T(8,128)(2,1)} async-done(((bf16[256,4096]{1,0:T(8,128)(2,1)}), bf16[256,1024]{1,0:T(8,128)(2,1)}) %reduce-scatter.2.cloned.1.call-update) | async-done | bytes 524304 | tf_op jit(solution)/shard_map/reduce_scatter | solution.py:166
  (65 shorter events, 6.9 us)
Async XLA Ops:
  6.5 20.5 %copy-start = (bf16[256,2048]{1,0:T(8,128)(2,1)S(1)}, bf16[256,2048]{1,0:T(8,128)(2,1)}, u32[]{:S(2)}) copy-start(bf16[256,2048]{1,0:T(8,128)(2,1)} %param.11) | copy-start | bytes 3145732
  6.5 108.9 %all-gather.2.cloned.1.call-start = ((), (), s32[]{:S(2)}) async-start(), calls=%async_computation.1 | async-start | bytes 17039360 | tf_op jit(solution)/shard_map/all_gather | solution.py:124
  7.3 156.1 %reduce-scatter.2.cloned.1.call-start = ((), (), s32[]{:S(2)}) async-start(), calls=%async_computation.2 | async-start | bytes 2621440 | tf_op jit(solution)/shard_map/reduce_scatter | solution.py:166
  9.6 11.6 %collective-permute-start = (bf16[3,2688]{1,0:T(4,128)(2,1)S(1)}, bf16[3,2688]{1,0:T(4,128)(2,1)S(1)}, u32[]{:S(2)}, u32[]{:S(2)}) collective-permute-start(bf16[3,2688]{1,0:T(4,128)(2,1)S(1)} %pad_maximum_fusion.2), channel_id=1, source_target_pairs={{0,4},{4,8},{8,12},{12,16},{16,20},{20,24},{24,28},{28,32},{32,36}... | collective-permute-start | bytes 48392 | tf_op jit(solution)/shard_map/ppermute | solution.py:20
  17.7 1.1 copy-start.2
  27.1 2.7 %copy-start.6 = (f32[32,256]{1,0:T(8,128)S(1)}, f32[32,256]{1,0:T(8,128)}, u32[]{:S(2)}) copy-start(f32[32,256]{1,0:T(8,128)} %param.14) | copy-start | bytes 98308
  31.4 19.6 %copy-start.7 = (s32[256]{0:T(256)S(1)}, s32[256]{0:T(256)}, u32[]{:S(2)}) copy-start(s32[256]{0:T(256)} %param.17) | copy-start | bytes 3076
  31.5 1.7 collective-permute-start.2
  31.6 1.5 collective-permute-start.1
  33.2 27.4 %copy-start.8 = (f32[2048]{0:T(1024)S(1)}, f32[2048]{0:T(1024)}, u32[]{:S(2)}) copy-start(f32[2048]{0:T(1024)} %param.20) | copy-start | bytes 24580
  33.4 27.7 %copy-start.3 = (f32[32,256]{1,0:T(8,128)S(1)}, f32[32,256]{1,0:T(8,128)}, u32[]{:S(2)}) copy-start(f32[32,256]{1,0:T(8,128)} %copy-done.2) | copy-start | bytes 98308
  33.4 27.7 %copy-start.5 = (f32[32,256]{1,0:T(8,128)S(1)}, f32[32,256]{1,0:T(8,128)}, u32[]{:S(2)}) copy-start(f32[32,256]{1,0:T(8,128)} %get-tuple-element.19) | copy-start | bytes 98308
  33.4 13.2 %collective-permute-start.3 = (bf16[16,64,128]{2,1,0:T(8,128)(2,1)S(1)}, bf16[16,64,128]{2,1,0:T(8,128)(2,1)S(1)}, u32[]{:S(2)}, u32[]{:S(2)}) collective-permute-start(bf16[16,64,128]{2,1,0:T(8,128)(2,1)S(1)} %get-tuple-element.9), channel_id=1, source_target_pairs={{0,8},{4,12},{8,16},{12,20},{16,24},{20,28},{24,32},{28,36},{32,40... | collective-permute-start | bytes 786440 | tf_op jit(solution)/shard_map/ppermute | solution.py:20
  46.8 9.5 %collective-permute-start.4 = (bf16[16,64,128]{2,1,0:T(8,128)(2,1)S(1)}, bf16[16,64,128]{2,1,0:T(8,128)(2,1)S(1)}, u32[]{:S(2)}, u32[]{:S(2)}) collective-permute-start(bf16[16,64,128]{2,1,0:T(8,128)(2,1)S(1)} %add_convert_fusion.1), channel_id=1, source_target_pairs={{0,8},{4,12},{8,16},{12,20},{16,24},{20,28},{24,32},{28,36},{32,40... | collective-permute-start | bytes 786440 | tf_op jit(solution)/shard_map/ppermute | solution.py:20
  56.5 7.8 %collective-permute-start.5 = (bf16[16,64,128]{2,1,0:T(8,128)(2,1)S(1)}, bf16[16,64,128]{2,1,0:T(8,128)(2,1)S(1)}, u32[]{:S(2)}, u32[]{:S(2)}) collective-permute-start(bf16[16,64,128]{2,1,0:T(8,128)(2,1)S(1)} %add_convert_fusion), channel_id=1, source_target_pairs={{0,8},{4,12},{8,16},{12,20},{16,24},{20,28},{24,32},{28,36},{32,40... | collective-permute-start | bytes 786440 | tf_op jit(solution)/shard_map/ppermute | solution.py:20
  64.5 7.9 %collective-permute-start.6 = (bf16[16,64,128]{2,1,0:T(8,128)(2,1)S(1)}, bf16[16,64,128]{2,1,0:T(8,128)(2,1)S(1)}, u32[]{:S(2)}, u32[]{:S(2)}) collective-permute-start(bf16[16,64,128]{2,1,0:T(8,128)(2,1)S(1)} %fusion.22), channel_id=1, source_target_pairs={{0,4},{4,0},{8,12},{12,8},{16,20},{20,16},{24,28},{28,24},{32,36},... | collective-permute-start | bytes 786440 | tf_op jit(solution)/shard_map/ppermute | solution.py:107
  72.4 0.8 copy-start.4
  72.4 0.8 copy-start.9
  76.8 2.2 %copy-start.1 = (bf16[256,2048]{1,0:T(8,128)(2,1)S(1)}, bf16[256,2048]{1,0:T(8,128)(2,1)}, u32[]{:S(2)}) copy-start(bf16[256,2048]{1,0:T(8,128)(2,1)} %param.13) | copy-start | bytes 3145732
Sparse Core Ops, SparseCore 0:
  10.1 105.2 all-gather.1
  133.6 29.6 reduce-scatter.1
where the time goes:
time: 171 us; the launch traced here: 170 us
  waiting for transfers between devices  82.4 us (48%)
  starting transfers between devices  24.1 us (14%)
  matrix products  23.8 us (14%)
  between operations  15.1 us (9%)
  other arithmetic  13.4 us (8%)
  local copies, waits for them, and re-layouts  11.4 us (7%)
    all_gather x1, waiting for transfers between devices, on_device(): weight = lax.all_gather(output_weight, 'seq', axis=1, tiled=True)  35.4 us
    reduce_scatter x1, waiting for transfers between devices, on_device(): lax.psum_scatter(partial_value.astype(jnp.bfloat16), 'head', scatter_dime...  29.8 us
    dot_general x1, matrix products, on_device(): partial_value = jnp.dot(normed, weight, preferred_element_type=jnp.float32)  18.1 us
    ppermute x4, starting transfers between devices, passed_along(): lax.ppermute(value, axis, [(source, source + steps) for source in range(i...  17 us
    ppermute x4, waiting for transfers between devices, passed_along(): lax.ppermute(value, axis, [(source, source + steps) for source in range(i...  15.5 us
    ppermute x1, starting transfers between devices, chain_states(): got = lax.ppermute(sent, 'seq', swap).astype(jnp.float32)  6.52 us
    dot_general x1, matrix products, reading(): return jnp.einsum('ihn,hpn->ihp', readers, held_state, precision=highest)  3.64 us
  transfers between devices with their start and end apart: 9, of which 6 were waited for; matrix products, arithmetic and copies ran while one was open for 18% of the time, Pallas kernels for 0%

commit v1 on v0

--- a/solution.py
+++ b/solution.py
@@ -121,7 +121,9 @@
     norm_gain,
     output_weight,
 ):
-    weight = lax.all_gather(output_weight, "seq", axis=1, tiled=True)
+    weight = jnp.concatenate(
+        lax.all_to_all(jnp.stack([output_weight] * lax.axis_size("seq")), "seq", 0, 0), axis=1
+    )
     margin = KERNEL - 1
     length = documents.shape[0]
     head_count = decay_exponent.shape[0]

time: 171 us -> 499 us (2.92)
  waiting for transfers between devices: 82.4 us -> 403 us
  starting transfers between devices: 24.1 us -> 33.7 us
    ppermute x4, waiting for transfers between devices: 15.5 us -> 363 us  [passed_along(): lax.ppermute(value, axis, [(source, source + steps) for source in range(i...]
    all_gather x1 -> x0, waiting for transfers between devices: 35.4 us -> none  [on_device(): weight = lax.all_gather(output_weight, 'seq', axis=1, tiled=True)]
    all_to_all x0 -> x1, starting transfers between devices: none -> 13.5 us  [on_device(): lax.all_to_all(jnp.stack([output_weight] * lax.axis_size('seq')), 'seq',...]
    reduce_scatter x1, waiting for transfers between devices: 29.8 us -> 38.7 us  [on_device(): lax.psum_scatter(partial_value.astype(jnp.bfloat16), 'head', scatter_dime...]
    another operation x1 -> x2, local copies, waits for them, and re-layouts: 0.01 us -> 6.72 us  [the longest x1 6.72 us: on_device(): jnp.stack([output_weight] * lax.axis_size('seq'))]
  transfers between devices with their start and end apart: 9 -> 9, of which waited for: 6 -> 6; matrix products, arithmetic and copies ran while one was open for 18% -> 4% of each run, Pallas kernels for 0% -> 0%
where the time goes in v1:
time: 499 us
  waiting for transfers between devices  403 us (81%)
  starting transfers between devices  33.7 us (7%)
  matrix products  23.8 us (5%)
  between operations  15.2 us (3%)
  local copies, waits for them, and re-layouts  12.6 us (3%)
  other arithmetic  10.5 us (2%)
    ppermute x4, waiting for transfers between devices, passed_along(): lax.ppermute(value, axis, [(source, source + steps) for source in range(i...  363 us
    reduce_scatter x1, waiting for transfers between devices, on_device(): lax.psum_scatter(partial_value.astype(jnp.bfloat16), 'head', scatter_dime...  38.7 us
    dot_general x1, matrix products, on_device(): partial_value = jnp.dot(normed, weight, preferred_element_type=jnp.float32)  18.1 us
    ppermute x4, starting transfers between devices, passed_along(): lax.ppermute(value, axis, [(source, source + steps) for source in range(i...  16.4 us
    all_to_all x1, starting transfers between devices, on_device(): lax.all_to_all(jnp.stack([output_weight] * lax.axis_size('seq')), 'seq',...  13.5 us
  transfers between devices with their start and end apart: 9, of which 6 were waited for; matrix products, arithmetic and copies ran while one was open for 4% of the time, Pallas kernels for 0%

profile of v1, /device:TPU:1, one launch (start us, length us, event | category | flops | bytes accessed | tf_op | source)
XLA Modules:
  0.0 498.6 jit_solution(13407632714855091330)
XLA Ops:
  6.5 6.7 %stack.2 = bf16[64,2048,64]{1,2,0:T(8,128)(2,1)} broadcast(bf16[2048,64]{0,1:T(8,128)(2,1)} %param.21), dimensions={1,2} | broadcast | bytes 17039360 | tf_op jit(solution)/shard_map/stack | solution.py:125
  13.3 13.5 %all-to-all-start = ((bf16[64,2048,64]{1,2,0:T(8,128)(2,1)}), bf16[64,2048,64]{1,2,0:T(8,128)(2,1)}, u32[]{:S(2)}, u32[]{:S(2)}) async-start(bf16[64,2048,64]{1,2,0:T(8,128)(2,1)} %stack.2), calls=%async_computation | async-start | bytes 33554432 | tf_op jit(solution)/shard_map/all_to_all | solution.py:125
  27.1 3.5 collective-permute-start
  30.7 0.6 reduce-window.6
  31.8 0.7 slice.157
  32.7 352.7 %collective-permute-done = bf16[3,2688]{1,0:T(4,128)(2,1)S(1)} collective-permute-done((bf16[3,2688]{1,0:T(4,128)(2,1)S(1)}, bf16[3,2688]{1,0:T(4,128)(2,1)S(1)}, u32[]{:S(2)}, u32[]{:S(2)}) %collective-permute-start) | collective-permute-done | bytes 16160 | tf_op jit(solution)/shard_map/ppermute | solution.py:20
  385.4 0.5 slice.155
  387.5 1.4 slice_compare_fusion.2
  388.9 2.1 multiply_convert_fusion
  391.0 0.5 copy.16
  391.7 0.7 multiply_convert_fusion.3
  392.6 0.7 multiply_bitcast_fusion.1
  393.3 0.5 broadcast_in_dim.115
  393.8 0.5 fusion.11
  394.5 0.5 collective-permute-start.1
  394.9 1.0 collective-permute-done.1
  396.2 4.6 collective-permute-start.3
  400.8 5.3 %collective-permute-done.3 = bf16[16,64,128]{2,1,0:T(8,128)(2,1)S(1)} collective-permute-done((bf16[16,64,128]{2,1,0:T(8,128)(2,1)S(1)}, bf16[16,64,128]{2,1,0:T(8,128)(2,1)S(1)}, u32[]{:S(2)}, u32[]{:S(2)}) %collective-permute-start.3) | collective-permute-done | bytes 262176 | tf_op jit(solution)/shard_map/ppermute | solution.py:20
  406.3 4.1 collective-permute-start.4
  410.6 4.3 collective-permute-done.4
  415.1 4.1 collective-permute-start.5
  419.4 0.3 fusion.34
  419.7 2.3 fusion.1
  422.0 0.8 collective-permute-done.5
  422.9 3.2 collective-permute-start.6
  426.1 1.4 fusion.35
  427.8 0.5 broadcast_in_dim.116
  428.3 3.6 fusion.3
  431.9 2.0 copy.26
  433.9 0.6 fusion.7
  435.0 18.1 %convolution_convert_fusion = bf16[256,4096]{1,0:T(8,128)(2,1)} fusion(bf16[2048,4096]{0,1:T(8,128)(2,1)} %bitcast.23, bf16[256,1024]{1,0:T(8,128)(2,1)S(1)} %get-tuple-element.12, bf16[256,1024]{1,0:T(8,128)(2,1)S(1)} %get-tuple-element.11), kind=kOutput, calls=%fused_computation.3 | convolution fusion | flops 4298113024 | bytes 19922944 | tf_op jit(solution)/shard_map/dot_general | solution.py:167
  453.1 38.7 %reduce-scatter.2.cloned.1.call-done = bf16[256,1024]{1,0:T(8,128)(2,1)} async-done(((bf16[256,4096]{1,0:T(8,128)(2,1)}), bf16[256,1024]{1,0:T(8,128)(2,1)}) %reduce-scatter.2.cloned.1.call-update) | async-done | bytes 524304 | tf_op jit(solution)/shard_map/reduce_scatter | solution.py:168
  (73 shorter events, 3.6 us)
Async XLA Ops:
  13.3 13.6 %copy-start.9 = (s32[256]{0:T(256)S(1)}, s32[256]{0:T(256)}, u32[]{:S(2)}) copy-start(s32[256]{0:T(256)} %param.17) | copy-start | bytes 3076
  13.3 13.7 %copy-start.4 = (bf16[256,2,256]{2,1,0:T(2,128)(2,1)S(1)}, bf16[256,2,256]{2,1,0:T(2,128)(2,1)}, u32[]{:S(2)}) copy-start(bf16[256,2,256]{2,1,0:T(2,128)(2,1)} %param.12) | copy-start | bytes 786436
  13.3 13.7 %copy-start = (bf16[256,2048]{1,0:T(8,128)(2,1)S(1)}, bf16[256,2048]{1,0:T(8,128)(2,1)}, u32[]{:S(2)}) copy-start(bf16[256,2048]{1,0:T(8,128)(2,1)} %param.11) | copy-start | bytes 3145732
  13.3 17.4 %copy-start.13 = (f32[32]{0:T(128)S(1)}, f32[32]{0:T(128)}, u32[]{:S(2)}) copy-start(f32[32]{0:T(128)} %param.15) | copy-start | bytes 388
  13.3 17.4 %copy-start.7 = (f32[32,256]{1,0:T(8,128)S(1)}, f32[32,256]{1,0:T(8,128)}, u32[]{:S(2)}) copy-start(f32[32,256]{1,0:T(8,128)} %param.14) | copy-start | bytes 98308
  13.3 18.2 %copy-start.10 = (f32[4,2,256]{2,1,0:T(2,128)S(1)}, f32[4,2,256]{2,1,0:T(2,128)}, u32[]{:S(2)}) copy-start(f32[4,2,256]{2,1,0:T(2,128)} %param.19) | copy-start | bytes 24580
  13.3 18.3 %copy-start.8 = (f32[4,2048]{1,0:T(4,128)S(1)}, f32[4,2048]{1,0:T(4,128)}, u32[]{:S(2)}) copy-start(f32[4,2048]{1,0:T(4,128)} %param.18) | copy-start | bytes 98308
  13.3 421.7 %all-to-all-start = ((bf16[64,2048,64]{1,2,0:T(8,128)(2,1)}), bf16[64,2048,64]{1,2,0:T(8,128)(2,1)}, u32[]{:S(2)}, u32[]{:S(2)}) async-start(bf16[64,2048,64]{1,2,0:T(8,128)(2,1)} %stack.2), calls=%async_computation | async-start | bytes 33554432 | tf_op jit(solution)/shard_map/all_to_all | solution.py:125
  26.8 465.0 %reduce-scatter.2.cloned.1.call-start = ((), (), s32[]{:S(2)}) async-start(), calls=%async_computation.2 | async-start | bytes 2621440 | tf_op jit(solution)/shard_map/reduce_scatter | solution.py:168
  27.1 358.3 %collective-permute-start = (bf16[3,2688]{1,0:T(4,128)(2,1)S(1)}, bf16[3,2688]{1,0:T(4,128)(2,1)S(1)}, u32[]{:S(2)}, u32[]{:S(2)}) collective-permute-start(bf16[3,2688]{1,0:T(4,128)(2,1)S(1)} %pad_maximum_fusion.2), channel_id=1, source_target_pairs={{0,4},{4,8},{8,12},{12,16},{16,20},{20,24},{24,28},{28,32},{32,36}... | collective-permute-start | bytes 48392 | tf_op jit(solution)/shard_map/ppermute | solution.py:20
  31.6 357.3 %copy-start.2 = (f32[32,256]{1,0:T(8,128)}, f32[32,256]{1,0:T(8,128)S(1)}, u32[]{:S(2)}) copy-start(f32[32,256]{1,0:T(8,128)S(1)} %copy_bitcast_fusion) | copy-start | bytes 98308
  394.3 1.7 collective-permute-start.2
  394.5 1.5 collective-permute-start.1
  396.0 23.2 %copy-start.11 = (f32[2048]{0:T(1024)S(1)}, f32[2048]{0:T(1024)}, u32[]{:S(2)}) copy-start(f32[2048]{0:T(1024)} %param.20) | copy-start | bytes 24580
  396.2 23.4 %copy-start.3 = (f32[32,256]{1,0:T(8,128)S(1)}, f32[32,256]{1,0:T(8,128)}, u32[]{:S(2)}) copy-start(f32[32,256]{1,0:T(8,128)} %copy-done.2) | copy-start | bytes 98308
  396.2 23.4 %copy-start.6 = (f32[32,256]{1,0:T(8,128)S(1)}, f32[32,256]{1,0:T(8,128)}, u32[]{:S(2)}) copy-start(f32[32,256]{1,0:T(8,128)} %get-tuple-element.19) | copy-start | bytes 98308
  396.2 9.9 %collective-permute-start.3 = (bf16[16,64,128]{2,1,0:T(8,128)(2,1)S(1)}, bf16[16,64,128]{2,1,0:T(8,128)(2,1)S(1)}, u32[]{:S(2)}, u32[]{:S(2)}) collective-permute-start(bf16[16,64,128]{2,1,0:T(8,128)(2,1)S(1)} %get-tuple-element.9), channel_id=1, source_target_pairs={{0,8},{4,12},{8,16},{12,20},{16,24},{20,28},{24,32},{28,36},{32,40... | collective-permute-start | bytes 786440 | tf_op jit(solution)/shard_map/ppermute | solution.py:20
  406.3 8.5 %collective-permute-start.4 = (bf16[16,64,128]{2,1,0:T(8,128)(2,1)S(1)}, bf16[16,64,128]{2,1,0:T(8,128)(2,1)S(1)}, u32[]{:S(2)}, u32[]{:S(2)}) collective-permute-start(bf16[16,64,128]{2,1,0:T(8,128)(2,1)S(1)} %add_convert_fusion.1), channel_id=1, source_target_pairs={{0,8},{4,12},{8,16},{12,20},{16,24},{20,28},{24,32},{28,36},{32,40... | collective-permute-start | bytes 786440 | tf_op jit(solution)/shard_map/ppermute | solution.py:20
  415.1 7.7 %collective-permute-start.5 = (bf16[16,64,128]{2,1,0:T(8,128)(2,1)S(1)}, bf16[16,64,128]{2,1,0:T(8,128)(2,1)S(1)}, u32[]{:S(2)}, u32[]{:S(2)}) collective-permute-start(bf16[16,64,128]{2,1,0:T(8,128)(2,1)S(1)} %add_convert_fusion), channel_id=1, source_target_pairs={{0,8},{4,12},{8,16},{12,20},{16,24},{20,28},{24,32},{28,36},{32,40... | collective-permute-start | bytes 786440 | tf_op jit(solution)/shard_map/ppermute | solution.py:20
  422.9 4.6 collective-permute-start.6
  427.5 0.8 copy-start.5
  427.5 0.8 copy-start.12
  431.9 2.0 copy-start.1
Sparse Core Ops, SparseCore 0:
  453.2 38.5 reduce-scatter.1
